TPU v7x, 32 devices: a whole 2x2x4 slice. The times are simulated.
32 devices in a mesh: dp: 16 (over z, y, core), tensor: 2 (over x).
Axes of the slice: x: 2, y: 2, z: 4, core: 2. Of those that a mesh axis runs over, the one named last changes fastest.
Arguments:
- frames: bfloat16 [16384, 2048], P('dp', 'tensor'), may hold values from -16 to 16
- gain: bfloat16 [2048], P('tensor'), may hold values from 0.099609375 to 1.8984375
- w_first: bfloat16 [32, 64, 128], P('tensor'), may hold values from -0.75 to 0.75
- w_second: bfloat16 [128, 32, 64], P('tensor'), may hold values from -1 to 1
- w_third: bfloat16 [128, 64, 32], P('tensor'), may hold values from -0.75 to 0.75
- w_fourth: bfloat16 [32, 128, 64], P('tensor'), may hold values from -0.5 to 0.5
- cotangent: bfloat16 [16384, 2048], P('dp', 'tensor'), may hold values from -6 to 6
Outputs:
- output: bfloat16 [16384, 2048], P('dp', 'tensor')
- input_gradient: bfloat16 [16384, 2048], P('dp', 'tensor')
- grad_first: float32 [32, 64, 128], P('tensor')
- grad_second: float32 [128, 32, 64], P('tensor')
- grad_third: float32 [128, 64, 32], P('tensor')
- grad_fourth: float32 [32, 128, 64], P('tensor')
- grad_gain: float32 [2048], P('tensor')
All inputs are finite; a program needn't handle non-finite values.
Results may differ from a plain program's by a relative error of at most 0.0072.
Values may be sent and summed in bfloat16 or wider, within the bound.
A program may use at most 128 MiB of HBM per device.

v0:
```python
import math

import jax
import jax.numpy as jnp
from jax import lax
from jax.sharding import PartitionSpec as P

BLOCK_FEATURES = 64
MODEL_WIDTH = 2048


def gelu_parts(value):
    cdf = 0.5 * (1.0 + jax.scipy.special.erf(value * 0.7071067811865476))
    pdf = jnp.exp(-0.5 * value * value) * 0.3989422804014327
    return (value * cdf, cdf + value * pdf)


def block_path(frames, gain, w_first, w_second, w_third, w_fourth, cotangent):
    single_float = jnp.float32
    brain_float_half = jnp.bfloat16
    frame_row_count = frames.shape[0]
    model_width_blocks = w_first.shape[0]
    input_float = frames.astype(single_float)
    gain_wide_float = gain.astype(single_float)
    row_sum, row_square = lax.psum(
        (jnp.sum(input_float, 1), jnp.sum(input_float * input_float, 1)), "tensor"
    )
    row_mean_value = (row_sum / MODEL_WIDTH)[:, None]
    msq = (row_square / MODEL_WIDTH)[:, None]
    inverse_deviation = 1.0 / jnp.sqrt(msq - row_mean_value * row_mean_value + 1e-05)
    centered_input = (input_float - row_mean_value) * inverse_deviation
    normalized_rows = (
        (centered_input * gain_wide_float)
        .astype(brain_float_half)
        .reshape(frame_row_count, model_width_blocks, BLOCK_FEATURES)
    )
    lifted = jnp.einsum(
        "tai,aim->amt", normalized_rows, w_first, preferred_element_type=single_float
    ).astype(brain_float_half)
    received = lax.all_to_all(lifted, "tensor", split_axis=1, concat_axis=0, tiled=True)
    mixed = jnp.einsum("amt,maq->mqt", received, w_second, preferred_element_type=single_float)
    act, slope = gelu_parts(mixed)
    act_b = act.astype(brain_float_half)
    folded = jnp.einsum("mqt,mqp->mpt", act_b, w_third, preferred_element_type=single_float).astype(
        brain_float_half
    )
    spread_lift, slope, act_b, folded = (received, slope, act_b, folded)
    received = lax.all_to_all(folded, "tensor", split_axis=1, concat_axis=0, tiled=True)
    back = jnp.einsum("mat,ami->ait", received, w_fourth, preferred_element_type=single_float)
    owned_fold, back = (received, back)
    back_rows = jnp.transpose(back, (2, 0, 1)).reshape(
        frame_row_count, model_width_blocks * BLOCK_FEATURES
    )
    output = (input_float + 0.5 * back_rows).astype(brain_float_half)
    scale = 1.0 / math.sqrt(frame_row_count * lax.axis_size("dp"))
    grad_out = (
        (0.5 * cotangent.astype(single_float))
        .astype(brain_float_half)
        .reshape(frame_row_count, model_width_blocks, BLOCK_FEATURES)
    )
    g_fourth = jnp.einsum("mat,tai->ami", owned_fold, grad_out, preferred_element_type=single_float)
    dfold_local = jnp.einsum(
        "tai,ami->mat", grad_out, w_fourth, preferred_element_type=single_float
    ).astype(brain_float_half)
    dfold = lax.all_to_all(dfold_local, "tensor", split_axis=0, concat_axis=1, tiled=True)
    g_third = jnp.einsum("mqt,mpt->mqp", act_b, dfold, preferred_element_type=single_float)
    dmix = (
        jnp.einsum("mpt,mqp->mqt", dfold, w_third, preferred_element_type=single_float) * slope
    ).astype(brain_float_half)
    g_second = jnp.einsum("amt,mqt->maq", spread_lift, dmix, preferred_element_type=single_float)
    dlift_local = jnp.einsum(
        "mqt,maq->amt", dmix, w_second, preferred_element_type=single_float
    ).astype(brain_float_half)
    dlift = lax.all_to_all(dlift_local, "tensor", split_axis=0, concat_axis=1, tiled=True)
    g_first = jnp.einsum(
        "tai,amt->aim", normalized_rows, dlift, preferred_element_type=single_float
    )
    normed_gradient = jnp.einsum(
        "amt,aim->tai", dlift, w_first, preferred_element_type=single_float
    ).reshape(frame_row_count, model_width_blocks * BLOCK_FEATURES)
    gain_gradient = jnp.sum(normed_gradient * centered_input, 0)
    expected_gradient = normed_gradient * gain_wide_float
    gradient_sum, gradient_centered_sum = lax.psum(
        (jnp.sum(expected_gradient, 1), jnp.sum(expected_gradient * centered_input, 1)), "tensor"
    )
    input_gradient = (
        cotangent.astype(single_float)
        + inverse_deviation
        * (
            expected_gradient
            - (gradient_sum / MODEL_WIDTH)[:, None]
            - centered_input * (gradient_centered_sum / MODEL_WIDTH)[:, None]
        )
    ).astype(brain_float_half)
    sum_first, sum_second, sum_third, sum_fourth, sum_gain = lax.psum(
        (
            g_first * scale,
            g_second * scale,
            g_third * scale,
            g_fourth * scale,
            gain_gradient * scale,
        ),
        "dp",
    )
    return (output, input_gradient, sum_first, sum_second, sum_third, sum_fourth, sum_gain)


def per_device(frames, gain, w_first, w_second, w_third, w_fourth, cotangent):
    return block_path(frames, gain, w_first, w_second, w_third, w_fourth, cotangent)


def solution(mesh):
    in_specs = (
        P("dp", "tensor"),
        P("tensor"),
        P("tensor", None, None),
        P("tensor", None, None),
        P("tensor", None, None),
        P("tensor", None, None),
        P("dp", "tensor"),
    )
    out_specs = (
        P("dp", "tensor"),
        P("dp", "tensor"),
        P("tensor", None, None),
        P("tensor", None, None),
        P("tensor", None, None),
        P("tensor", None, None),
        P("tensor"),
    )
    return jax.shard_map(
        per_device, mesh=mesh, in_specs=in_specs, out_specs=out_specs, check_vma=False
    )
```

profile of v0, /device:TPU:0, one launch (start us, length us, event | category | flops | bytes accessed | tf_op | source)
XLA Modules:
  0.0 390.5 jit_solution(5932159126581588593)
XLA Ops:
  7.2 2.9 copy.35
  10.8 5.9 %all-reduce.2 = (f32[1024]{0:T(1024)S(1)}, f32[1024]{0:T(1024)S(1)}) all-reduce(f32[1024]{0:T(1024)S(1)} %get-tuple-element.24, f32[1024]{0:T(1024)S(1)} %get-tuple-element.23), channel_id=1, replica_groups=mesh['dp'=16,'tensor'=2] {'tensor'}, use_global_device_ids=true, to_apply=%region_3.0 | all-reduce | flops 2048 | bytes 16384 | tf_op jit(solution)/shard_map/psum | solution.py:25
  17.3 1.3 copy-done.6
  18.7 3.3 convert_bitcast_fusion.3
  22.0 6.8 %copy.36 = bf16[16,128,1024]{2,0,1:T(8,128)(2,1)} copy(bf16[16,128,1024]{1,2,0:T(8,128)(2,1)} %convert_bitcast_fusion.3) | data formatting | bytes 8388608 | tf_op jit(solution)/shard_map/convert_element_type | solution.py:39
  28.8 5.6 %all-to-all-start = ((bf16[16,128,1024]{2,0,1:T(8,128)(2,1)}), bf16[16,128,1024]{2,0,1:T(8,128)(2,1)}, u32[]{:S(2)}, u32[]{:S(2)}) async-start(bf16[16,128,1024]{2,0,1:T(8,128)(2,1)} %copy.36), calls=%async_computation | async-start | bytes 8388608 | tf_op jit(solution)/shard_map/all_to_all | solution.py:40
  34.4 4.0 %copy.41 = bf16[1024,1024]{0,1:T(8,128)(2,1)} copy(bf16[1024,1024]{1,0:T(8,128)(2,1)} %param.13) | data formatting | bytes 4194304 | tf_op args[6]
  38.4 2.1 fusion.10
  40.5 1.4 copy-done.8
  41.8 3.3 convert_bitcast_fusion.1
  45.1 6.9 %copy.42 = bf16[128,16,1024]{2,1,0:T(8,128)(2,1)} copy(bf16[128,16,1024]{0,2,1:T(8,128)(2,1)} %convert_bitcast_fusion.1) | data formatting | bytes 8388608 | tf_op jit(solution)/shard_map/convert_element_type | solution.py:64
  52.0 29.2 %all-to-all-done = bf16[16,128,1024]{2,0,1:T(8,128)(2,1)} async-done(((bf16[16,128,1024]{2,0,1:T(8,128)(2,1)}), bf16[16,128,1024]{2,0,1:T(8,128)(2,1)}, u32[]{:S(2)}, u32[]{:S(2)}) %all-to-all-start) | async-done | bytes 4194336 | tf_op jit(solution)/shard_map/all_to_all | solution.py:40
  81.2 5.8 %all-to-all-start.2 = ((bf16[128,16,1024]{2,1,0:T(8,128)(2,1)}), bf16[128,16,1024]{2,1,0:T(8,128)(2,1)}, u32[]{:S(2)}, u32[]{:S(2)}) async-start(bf16[128,16,1024]{2,1,0:T(8,128)(2,1)} %copy.42), calls=%async_computation.2 | async-start | bytes 8388608 | tf_op jit(solution)/shard_map/all_to_all | solution.py:65
  87.0 5.0 %copy.38 = bf16[2,16,64,1024]{3,1,0,2:T(8,128)(2,1)} copy(bf16[2,16,64,1024]{3,1,2,0:T(8,128)(2,1)} %bitcast.4) | data formatting | bytes 8388608 | tf_op jit(solution)/shard_map/all_to_all | solution.py:40
  92.0 40.6 %all-to-all-done.2 = bf16[128,16,1024]{2,1,0:T(8,128)(2,1)} async-done(((bf16[128,16,1024]{2,1,0:T(8,128)(2,1)}), bf16[128,16,1024]{2,1,0:T(8,128)(2,1)}, u32[]{:S(2)}, u32[]{:S(2)}) %all-to-all-start.2) | async-done | bytes 4194336 | tf_op jit(solution)/shard_map/all_to_all | solution.py:65
  132.6 5.1 %copy.43 = bf16[64,2,16,1024]{3,2,1,0:T(8,128)(2,1)} copy(bf16[64,2,16,1024]{3,2,0,1:T(8,128)(2,1)} %bitcast.16) | data formatting | bytes 8388608 | tf_op jit(solution)/shard_map/all_to_all | solution.py:65
  137.8 8.7 %fusion.9 = (bf16[64,64,1024]{2,1,0:T(8,128)(2,1)S(1)}, f32[64,1024,64]{1,2,0:T(8,128)}) fusion(bf16[32,64,1024]{2,0,1:T(8,128)(2,1)S(1)} %bitcast.85, bf16[64,32,64]{2,1,0:T(8,128)(2,1)S(1)} %copy-done), kind=kOutput, calls=%fused_computation.12 | convolution fusion | flops 289406976 | bytes 29622272 | tf_op jit(solution)/shard_map/amt,maq->mqt/dot_general | solution.py:41
  146.5 1.2 convert_bitcast_fusion.2
  147.7 2.0 copy-done.1
  149.7 4.3 %copy.39 = bf16[64,32,1024]{2,0,1:T(8,128)(2,1)} copy(bf16[64,32,1024]{2,1,0:T(8,128)(2,1)S(1)} %convert_bitcast_fusion.2) | data formatting | bytes 8388608 | tf_op jit(solution)/shard_map/convert_element_type | solution.py:44
  154.0 5.6 %all-to-all-start.1 = ((bf16[64,32,1024]{2,0,1:T(8,128)(2,1)}), bf16[64,32,1024]{2,0,1:T(8,128)(2,1)}, u32[]{:S(2)}, u32[]{:S(2)}) async-start(bf16[64,32,1024]{2,0,1:T(8,128)(2,1)} %copy.39), calls=%async_computation.1 | async-start | bytes 8388608 | tf_op jit(solution)/shard_map/all_to_all | solution.py:48
  159.6 11.2 %fusion.5 = bf16[64,64,1024]{2,1,0:T(8,128)(2,1)S(1)} fusion(f32[64,1024,64]{1,2,0:T(8,128)} %get-tuple-element.40, bf16[64,32,1024]{2,1,0:T(8,128)(2,1)} %bitcast.94, bf16[64,64,32]{1,2,0:T(8,128)(2,1)} %param.11), kind=kOutput, calls=%fused_computation.6 | convolution fusion | flops 310378496 | bytes 29622272 | tf_op jit(solution)/shard_map/mpt,mqp->mqt/dot_general | solution.py:68
  170.8 1.3 convert_bitcast_fusion
  172.1 1.9 copy-done.5
  174.0 4.3 %copy.44 = bf16[32,64,1024]{2,1,0:T(8,128)(2,1)} copy(bf16[32,64,1024]{2,0,1:T(8,128)(2,1)S(1)} %convert_bitcast_fusion) | data formatting | bytes 8388608 | tf_op jit(solution)/shard_map/convert_element_type | solution.py:73
  178.3 26.2 %all-to-all-done.1 = bf16[64,32,1024]{2,0,1:T(8,128)(2,1)} async-done(((bf16[64,32,1024]{2,0,1:T(8,128)(2,1)}), bf16[64,32,1024]{2,0,1:T(8,128)(2,1)}, u32[]{:S(2)}, u32[]{:S(2)}) %all-to-all-start.1) | async-done | bytes 4194336 | tf_op jit(solution)/shard_map/all_to_all | solution.py:48
  204.5 5.6 %all-to-all-start.3 = ((bf16[32,64,1024]{2,1,0:T(8,128)(2,1)}), bf16[32,64,1024]{2,1,0:T(8,128)(2,1)}, u32[]{:S(2)}, u32[]{:S(2)}) async-start(bf16[32,64,1024]{2,1,0:T(8,128)(2,1)} %copy.44), calls=%async_computation.3 | async-start | bytes 8388608 | tf_op jit(solution)/shard_map/all_to_all | solution.py:74
  210.4 8.1 %convolution_multiply_fusion.1 = f32[64,32,64]{2,1,0:T(8,128)} fusion(bf16[32,64,1024]{2,0,1:T(8,128)(2,1)} %bitcast.84, bf16[64,64,1024]{2,1,0:T(8,128)(2,1)} %copy-done.5), kind=kOutput, calls=%fused_computation.41 | convolution fusion | flops 268566528 | bytes 13107200 | tf_op jit(solution)/shard_map/amt,mqt->maq/dot_general | solution.py:70
  218.5 7.0 %convolution_multiply_fusion.2 = f32[64,64,32]{1,2,0:T(8,128)} fusion(bf16[64,64,1024]{2,1,0:T(8,128)(2,1)} %copy-done.1, bf16[64,32,1024]{2,1,0:T(8,128)(2,1)S(1)} %bitcast.95), kind=kOutput, calls=%fused_computation.42 | convolution fusion | flops 268566528 | bytes 13107200 | tf_op jit(solution)/shard_map/mqt,mpt->mqp/dot_general | solution.py:66
  225.5 2.8 copy.40
  228.3 2.3 convolution_multiply_fusion.3
  230.7 2.7 convolution_multiply_fusion
  233.4 20.8 %all-to-all-done.3 = bf16[32,64,1024]{2,1,0:T(8,128)(2,1)} async-done(((bf16[32,64,1024]{2,1,0:T(8,128)(2,1)}), bf16[32,64,1024]{2,1,0:T(8,128)(2,1)}, u32[]{:S(2)}, u32[]{:S(2)}) %all-to-all-start.3) | async-done | bytes 4194336 | tf_op jit(solution)/shard_map/all_to_all | solution.py:74
  254.2 2.8 copy.45
  256.9 2.0 copy-done.4
  258.9 2.3 convolution_multiply_fusion.4
  261.2 2.9 fusion.24
  264.2 2.0 copy-done.3
  266.1 1.2 fusion.21
  267.4 5.0 %all-reduce.1 = (f32[1024]{0:T(1024)S(1)}, f32[1024]{0:T(1024)S(1)}) all-reduce(f32[1024]{0:T(1024)S(1)} %get-tuple-element.22, f32[1024]{0:T(1024)S(1)} %get-tuple-element.37), channel_id=1, replica_groups=mesh['dp'=16,'tensor'=2] {'tensor'}, use_global_device_ids=true, to_apply=%region_7.0 | all-reduce | flops 2048 | bytes 16384 | tf_op jit(solution)/shard_map/psum | solution.py:83
  272.4 6.5 %fusion.11 = (bf16[1024,1024]{0,1:T(8,128)(2,1)}, bf16[1024,1024]{0,1:T(8,128)(2,1)}) fusion(bf16[1024,1024]{0,1:T(8,128)(2,1)} %copy.41, bf16[1024,1024]{0,1:T(8,128)(2,1)S(1)} %copy.35, f32[16,1024,64]{1,2,0:T(8,128)} %copy-done.3, f32[1024]{0:T(1024)S(1)} %get-tuple-element.41, f32[1024]{0:T(1024)S(1)} %get-tuple-element.42, ...), kind=kLoop, calls=%fused_computation.20 | loop fusion | flops 13631488 | bytes 16797696 | tf_op jit(solution)/shard_map/convert_element_type | solution.py:94
  278.9 4.1 %copy.46 = bf16[1024,1024]{1,0:T(8,128)(2,1)} copy(bf16[1024,1024]{0,1:T(8,128)(2,1)} %get-tuple-element.34) | data formatting | bytes 4194304
  283.0 2.5 copy.47
  285.6 30.5 %psum.71 = f32[1024]{0:T(1024)} all-reduce(f32[1024]{0:T(1024)S(1)} %broadcast_multiply_fusion), channel_id=1, replica_groups=mesh['dp'=16,'tensor'=2] {'dp'}, use_global_device_ids=true, to_apply=%region_13.0 | all-reduce | flops 1024 | bytes 8192 | tf_op jit(solution)/shard_map/psum | solution.py:95
  316.1 60.3 %all-reduce.5.cloned.1.call-done = (f32[16,64,128]{2,1,0:T(8,128)}, f32[64,32,64]{2,1,0:T(8,128)}, f32[64,64,32]{1,2,0:T(8,128)}, f32[16,128,64]{1,2,0:T(8,128)}) async-done(((f32[16,64,128]{2,1,0:T(8,128)}, f32[64,32,64]{2,1,0:T(8,128)}, f32[64,64,32]{1,2,0:T(8,128)}, f32[16,128,64]{1,2,0:T(8,128)}), (f32[16,64,128]{2,1,0:T(8,128)}, f32[64,32,64]{2,1,0:T(8,128)}, f32[64,64,32]{1,2,0:T(8,128)}, ...) | async-done | bytes 2097168 | tf_op jit(solution)/shard_map/psum | solution.py:95
  376.4 1.9 copy.53
  378.3 2.3 copy.54
  380.6 2.3 copy.55
  (38 shorter events, 2.6 us)
Async XLA Ops:
  7.2 130.6 %copy-start = (bf16[64,32,64]{2,1,0:T(8,128)(2,1)S(1)}, bf16[64,32,64]{2,1,0:T(8,128)(2,1)}, u32[]{:S(2)}) copy-start(bf16[64,32,64]{2,1,0:T(8,128)(2,1)} %param.10) | copy-start | bytes 786436
  7.2 3.6 copy-start.16
  10.1 8.5 %copy-start.13 = (bf16[16,64,128]{2,1,0:T(8,128)(2,1)S(1)}, bf16[16,64,128]{2,1,0:T(8,128)(2,1)}, u32[]{:S(2)}) copy-start(bf16[16,64,128]{2,1,0:T(8,128)(2,1)} %param.9) | copy-start | bytes 786436
  17.3 1.3 copy-start.6
  28.8 52.4 %all-to-all-start = ((bf16[16,128,1024]{2,0,1:T(8,128)(2,1)}), bf16[16,128,1024]{2,0,1:T(8,128)(2,1)}, u32[]{:S(2)}, u32[]{:S(2)}) async-start(bf16[16,128,1024]{2,0,1:T(8,128)(2,1)} %copy.36), calls=%async_computation | async-start | bytes 8388608 | tf_op jit(solution)/shard_map/all_to_all | solution.py:40
  34.4 7.4 %copy-start.12 = (bf16[16,128,64]{1,2,0:T(8,128)(2,1)S(1)}, bf16[16,128,64]{1,2,0:T(8,128)(2,1)}, u32[]{:S(2)}) copy-start(bf16[16,128,64]{1,2,0:T(8,128)(2,1)} %param.12) | copy-start | bytes 786436
  40.4 1.4 copy-start.8
  81.2 51.5 %all-to-all-start.2 = ((bf16[128,16,1024]{2,1,0:T(8,128)(2,1)}), bf16[128,16,1024]{2,1,0:T(8,128)(2,1)}, u32[]{:S(2)}, u32[]{:S(2)}) async-start(bf16[128,16,1024]{2,1,0:T(8,128)(2,1)} %copy.42), calls=%async_computation.2 | async-start | bytes 8388608 | tf_op jit(solution)/shard_map/all_to_all | solution.py:65
  132.6 5.1 %copy-start.2 = (bf16[2,16,64,1024]{3,1,0,2:T(8,128)(2,1)S(1)}, bf16[2,16,64,1024]{3,1,0,2:T(8,128)(2,1)}, u32[]{:S(2)}) copy-start(bf16[2,16,64,1024]{3,1,0,2:T(8,128)(2,1)} %copy.38) | copy-start | bytes 12582916
  137.8 8.7 %copy-start.14 = (bf16[64,64,32]{1,2,0:T(8,128)(2,1)S(1)}, bf16[64,64,32]{1,2,0:T(8,128)(2,1)}, u32[]{:S(2)}) copy-start(bf16[64,64,32]{1,2,0:T(8,128)(2,1)} %param.11) | copy-start | bytes 786436
  146.5 3.2 copy-start.1
  154.0 50.6 %all-to-all-start.1 = ((bf16[64,32,1024]{2,0,1:T(8,128)(2,1)}), bf16[64,32,1024]{2,0,1:T(8,128)(2,1)}, u32[]{:S(2)}, u32[]{:S(2)}) async-start(bf16[64,32,1024]{2,0,1:T(8,128)(2,1)} %copy.39), calls=%async_computation.1 | async-start | bytes 8388608 | tf_op jit(solution)/shard_map/all_to_all | solution.py:48
  170.8 3.2 copy-start.5
  204.5 49.6 %all-to-all-start.3 = ((bf16[32,64,1024]{2,1,0:T(8,128)(2,1)}), bf16[32,64,1024]{2,1,0:T(8,128)(2,1)}, u32[]{:S(2)}, u32[]{:S(2)}) async-start(bf16[32,64,1024]{2,1,0:T(8,128)(2,1)} %copy.44), calls=%async_computation.3 | async-start | bytes 8388608 | tf_op jit(solution)/shard_map/all_to_all | solution.py:74
  210.1 166.2 %all-reduce.5.cloned.1.call-start = ((), (), s32[]{:S(2)}) async-start(), calls=%async_computation.4 | async-start | bytes 6291456 | tf_op jit(solution)/shard_map/psum | solution.py:95
  210.4 8.1 %copy-start.10 = (bf16[64,2,16,1024]{3,2,1,0:T(8,128)(2,1)S(1)}, bf16[64,2,16,1024]{3,2,1,0:T(8,128)(2,1)}, u32[]{:S(2)}) copy-start(bf16[64,2,16,1024]{3,2,1,0:T(8,128)(2,1)} %copy.43) | copy-start | bytes 12582916
  225.5 2.9 copy-start.9
  254.2 4.7 %copy-start.7 = (bf16[1024,1024]{0,1:T(8,128)(2,1)S(1)}, bf16[1024,1024]{0,1:T(8,128)(2,1)}, u32[]{:S(2)}) copy-start(bf16[1024,1024]{0,1:T(8,128)(2,1)} %copy-done.6) | copy-start | bytes 6291460
  256.9 2.0 copy-start.4
  264.2 2.0 copy-start.3
  278.9 4.1 %copy-start.11 = (bf16[1024,1024]{0,1:T(8,128)(2,1)S(1)}, bf16[1024,1024]{0,1:T(8,128)(2,1)}, u32[]{:S(2)}) copy-start(bf16[1024,1024]{0,1:T(8,128)(2,1)} %get-tuple-element.33) | copy-start | bytes 6291460
  376.4 6.5 %copy-start.15 = (f32[16,128,64]{1,2,0:T(8,128)S(1)}, f32[16,128,64]{1,2,0:T(8,128)}, u32[]{:S(2)}) copy-start(f32[16,128,64]{1,2,0:T(8,128)} %get-tuple-element.48) | copy-start | bytes 1572868
Sparse Core Ops, SparseCore 0:
  272.5 103.8 all-reduce.4
where the time goes:
time: 392 us; the launch traced here: 390 us
  waiting for transfers between devices  177 us (45%)
  local copies, waits for them, and re-layouts  69.4 us (18%)
  matrix products  54.4 us (14%)
  blocking collectives  41.4 us (11%)
  starting transfers between devices  22.8 us (6%)
  between operations  14.2 us (4%)
  other arithmetic  11.1 us (3%)
    psum x1, waiting for transfers between devices, block_path(): lax.psum((g_first * scale, g_second * scale, g_third * scale, g_fourth *...  60.3 us
    all_to_all x1, waiting for transfers between devices, block_path(): lax.all_to_all(dfold_local, 'tensor', split_axis=0, concat_axis=1, tiled=...  40.6 us
    unnamed x42, local copies, waits for them, and re-layouts  31.4 us
    psum x1, blocking collectives, block_path(): lax.psum((g_first * scale, g_second * scale, g_third * scale, g_fourth *...  30.5 us
    all_to_all x1, waiting for transfers between devices, block_path(): lax.all_to_all(lifted, 'tensor', split_axis=1, concat_axis=0, tiled=True)  29.2 us
    all_to_all x1, waiting for transfers between devices, block_path(): lax.all_to_all(folded, 'tensor', split_axis=1, concat_axis=0, tiled=True)  26.2 us
    all_to_all x1, waiting for transfers between devices, block_path(): lax.all_to_all(dlift_local, 'tensor', split_axis=0, concat_axis=1, tiled=...  20.8 us
    dot_general x1, matrix products, block_path(): jnp.einsum('mpt,mqp->mqt', dfold, w_third, preferred_element_type=single_...  11.2 us
  transfers between devices with their start and end apart: 5, of which 5 were waited for; matrix products, arithmetic and copies ran while one was open for 19% of the time, Pallas kernels for 0%

commit v1 on v0

v1 whole, which is shorter than its diff:
```python
import math

import jax
import jax.numpy as jnp
from jax import lax
from jax.sharding import PartitionSpec as P

F32 = jnp.float32
BF16 = jnp.bfloat16
LANES = 128


def gelu_parts(value):
    cdf = 0.5 * (1.0 + jax.scipy.special.erf(value * 0.7071067811865476))
    pdf = jnp.exp(-0.5 * value * value) * 0.3989422804014327
    return (value * cdf, cdf + value * pdf)


def dot32(spec, a, b):
    return jnp.einsum(spec, a, b, preferred_element_type=F32)


def swap_in(x, n):
    t, d = x.shape
    parts = lax.all_to_all(x.reshape(n, t // n, d), "tensor", 0, 0)
    return jnp.transpose(parts, (0, 2, 1)).reshape(n * d, t // n)


def swap_out(x, n):
    d, t = x.shape
    parts = jnp.transpose(x.reshape(n, d // n, t), (0, 2, 1))
    return lax.all_to_all(parts, "tensor", 0, 0).reshape(n * t, d // n)


def to_rows(g, n):
    b, r, c = g.shape
    k = LANES // c
    g = g.reshape(n, b // n, r, c)
    step = b // n // k
    if k > 1:
        g = jnp.concatenate([g[:, i * step : (i + 1) * step] for i in range(k)], axis=-1)
    return g.reshape(n, step * r, LANES)


def from_rows(rows, b, r, c):
    k = LANES // c
    g = rows.reshape(b // k, r, LANES)
    if k > 1:
        g = jnp.concatenate([g[:, :, i * c : (i + 1) * c] for i in range(k)], axis=0)
    return g


def tensor_sum(rows, n):
    got = lax.all_to_all(rows.astype(BF16), "tensor", 0, 0)
    return jnp.sum(got.astype(F32), 0)


def per_device(frames, gain, w_first, w_second, w_third, w_fourth, cotangent):
    n = lax.axis_size("tensor")
    dp = lax.axis_size("dp")
    a_loc, i_sz, m_sz = w_first.shape
    m_loc, a_sz, q_sz = w_second.shape
    width = a_sz * i_sz
    t_loc = frames.shape[0] // n

    x = swap_in(frames, n)
    w1 = lax.all_gather(w_first, "tensor", axis=0, tiled=True)
    gain_full = lax.all_gather(gain, "tensor", axis=0, tiled=True)
    w2 = lax.all_gather(w_second, "tensor", axis=0, tiled=True)
    cot = swap_in(cotangent, n)
    w3 = lax.all_gather(w_third, "tensor", axis=0, tiled=True)
    w4 = lax.all_gather(w_fourth, "tensor", axis=0, tiled=True)

    xf = x.astype(F32)
    gw = gain_full.astype(F32)[:, None]
    mean = jnp.sum(xf, 0, keepdims=True) / width
    msq = jnp.sum(xf * xf, 0, keepdims=True) / width
    rstd = 1.0 / jnp.sqrt(msq - mean * mean + 1e-05)
    xhat = (xf - mean) * rstd
    normed = (xhat * gw).astype(BF16).reshape(a_sz, i_sz, t_loc)
    lifted = dot32("ait,aim->amt", normed, w1).astype(BF16)
    mixed = dot32("amt,maq->mqt", lifted, w2)
    act, slope = gelu_parts(mixed)
    act = act.astype(BF16)
    folded = dot32("mqt,mqp->mpt", act, w3).astype(BF16)
    back = dot32("mat,ami->ait", folded, w4).reshape(width, t_loc)
    output = swap_out((xf + 0.5 * back).astype(BF16), n)

    dz = (0.5 * cot.astype(F32)).astype(BF16).reshape(a_sz, i_sz, t_loc)
    g4 = tensor_sum(to_rows(dot32("mat,ait->aim", folded, dz), n), n)
    dfold = dot32("ait,ami->mat", dz, w4).astype(BF16)
    g3 = tensor_sum(to_rows(dot32("mqt,mpt->mpq", act, dfold), n), n)
    dmix = (dot32("mpt,mqp->mqt", dfold, w3) * slope).astype(BF16)
    g2 = tensor_sum(to_rows(dot32("amt,mqt->maq", lifted, dmix), n), n)
    dlift = dot32("mqt,maq->amt", dmix, w2).astype(BF16)
    g1 = tensor_sum(to_rows(dot32("ait,amt->aim", normed, dlift), n), n)
    dn = dot32("amt,aim->ait", dlift, w1).reshape(width, t_loc)
    gg = jnp.sum(dn * xhat, 1)
    e = dn * gw
    e_mean = jnp.sum(e, 0, keepdims=True) / width
    ex_mean = jnp.sum(e * xhat, 0, keepdims=True) / width
    dx = (cot.astype(F32) + rstd * (e - e_mean - xhat * ex_mean)).astype(BF16)
    input_gradient = swap_out(dx, n)
    gg = jnp.sum(lax.all_to_all(gg.reshape(n, width // n), "tensor", 0, 0), 0)

    rows = jnp.concatenate([g1, g2, g3, g4, gg.reshape(-1, LANES)], 0)
    total = lax.psum(rows, "dp") * (1.0 / math.sqrt(frames.shape[0] * dp))
    r = g1.shape[0]
    s1 = from_rows(total[:r], a_loc, i_sz, m_sz)
    s2 = from_rows(total[r : 2 * r], m_loc, a_sz, q_sz)
    s3 = jnp.transpose(from_rows(total[2 * r : 3 * r], m_loc, a_sz, q_sz), (0, 2, 1))
    s4 = jnp.transpose(from_rows(total[3 * r : 4 * r], a_loc, i_sz, m_sz), (0, 2, 1))
    sg = total[4 * r :].reshape(-1)
    return (output, input_gradient, s1, s2, s3, s4, sg)


def solution(mesh):
    blocks = P("tensor", None, None)
    rows = P("dp", "tensor")
    return jax.shard_map(
        per_device,
        mesh=mesh,
        in_specs=(rows, P("tensor"), blocks, blocks, blocks, blocks, rows),
        out_specs=(rows, rows, blocks, blocks, blocks, blocks, P("tensor")),
        check_vma=False,
    )
```

time: 392 us -> 367 us (0.936)
  waiting for transfers between devices: 177 us -> 103 us
  blocking collectives: 41.4 us -> 69.6 us
  local copies, waits for them, and re-layouts: 69.4 us -> 42.4 us
  matrix products: 54.4 us -> 80.6 us
  starting transfers between devices: 22.8 us -> 36.7 us
  other arithmetic: 11.1 us -> 18.4 us
    all_to_all x4 -> x9, waiting for transfers between devices: 117 us -> 41.4 us  [the longest x2 26.8 us: swap_out(): return lax.all_to_all(parts, 'tensor', 0, 0).reshape(n * t, d // n)]
    all_gather x0 -> x5, blocking collectives: none -> 69.6 us  [the longest x1 26 us: per_device(): gain_full = lax.all_gather(gain, 'tensor', axis=0, tiled=True)]
    psum x3 -> x0, blocking collectives: 41.4 us -> none  [the longest x1 30.5 us: block_path(): lax.psum((g_first * scale, g_second * scale, g_third * scale, g_fourth *...]
    dot_general x12, matrix products: 54.4 us -> 80.6 us  [dot32(): return jnp.einsum(spec, a, b, preferred_element_type=F32)]
    unnamed x42 -> x44, local copies, waits for them, and re-layouts: 31.4 us -> 6.83 us
    all_to_all x4 -> x9, starting transfers between devices: 22.5 us -> 36.7 us  [the longest x4 15.7 us: tensor_sum(): got = lax.all_to_all(rows.astype(BF16), 'tensor', 0, 0)]
    reshape x0 -> x3, local copies, waits for them, and re-layouts: none -> 8.48 us  [the longest x2 7.88 us: swap_in(): parts = lax.all_to_all(x.reshape(n, t // n, d), 'tensor', 0, 0)]
    all_to_all x4 -> x3, local copies, waits for them, and re-layouts: 15.6 us -> 7.69 us  [the longest x2 6.29 us: swap_out(): return lax.all_to_all(parts, 'tensor', 0, 0).reshape(n * t, d // n)]
  transfers between devices with their start and end apart: 5 -> 10, of which waited for: 5 -> 7; matrix products, arithmetic and copies ran while one was open for 19% -> 16% of each run, Pallas kernels for 0% -> 0%
where the time goes in v1:
time: 367 us; the launch traced here: 365 us
  waiting for transfers between devices  103 us (28%)
  matrix products  80.6 us (22%)
  blocking collectives  69.6 us (19%)
  local copies, waits for them, and re-layouts  42.4 us (12%)
  starting transfers between devices  36.7 us (10%)
  other arithmetic  18.4 us (5%)
  between operations  14.3 us (4%)
    dot_general x12, matrix products, dot32(): return jnp.einsum(spec, a, b, preferred_element_type=F32)  80.6 us
    psum x1, waiting for transfers between devices, per_device(): total = lax.psum(rows, 'dp') * (1.0 / math.sqrt(frames.shape[0] * dp))  61.4 us
    all_to_all x2, waiting for transfers between devices, swap_out(): return lax.all_to_all(parts, 'tensor', 0, 0).reshape(n * t, d // n)  26.8 us
    all_gather x1, blocking collectives, per_device(): gain_full = lax.all_gather(gain, 'tensor', axis=0, tiled=True)  26 us
    all_to_all x4, starting transfers between devices, tensor_sum(): got = lax.all_to_all(rows.astype(BF16), 'tensor', 0, 0)  15.7 us
    all_gather x1, blocking collectives, per_device(): w3 = lax.all_gather(w_third, 'tensor', axis=0, tiled=True)  15 us
    all_gather x1, blocking collectives, per_device(): w2 = lax.all_gather(w_second, 'tensor', axis=0, tiled=True)  13.1 us
    all_to_all x2, starting transfers between devices, swap_in(): parts = lax.all_to_all(x.reshape(n, t // n, d), 'tensor', 0, 0)  9.17 us
  transfers between devices with their start and end apart: 10, of which 7 were waited for; matrix products, arithmetic and copies ran while one was open for 16% of the time, Pallas kernels for 0%

profile of v1, /device:TPU:0, one launch (start us, length us, event | category | flops | bytes accessed | tf_op | source)
XLA Modules:
  0.0 364.9 jit_solution(9955003560113710716)
XLA Ops:
  7.2 3.9 %copy.26 = bf16[2,512,1024]{1,2,0:T(8,128)(2,1)} copy(bf16[2,512,1024]{2,1,0:T(8,128)(2,1)} %bitcast.130) | data formatting | bytes 4194304 | tf_op jit(solution)/shard_map/reshape | solution.py:25
  11.1 4.3 %all-to-all-start = ((bf16[2,512,1024]{1,2,0:T(8,128)(2,1)}), bf16[2,512,1024]{1,2,0:T(8,128)(2,1)S(1)}, u32[]{:S(2)}, u32[]{:S(2)}) async-start(bf16[2,512,1024]{1,2,0:T(8,128)(2,1)} %copy.26), calls=%async_computation | async-start | bytes 4194304 | tf_op jit(solution)/shard_map/all_to_all | solution.py:25
  15.5 26.0 %all_gather.15 = bf16[2048]{0:T(1024)(128)(2,1)S(1)} all-gather(bf16[1024]{0:T(1024)(128)(2,1)S(1)} %copy-done.19), channel_id=1, replica_groups=mesh['dp'=16,'tensor'=2] {'tensor'}, dimensions={0}, use_global_device_ids=true | all-gather | bytes 6144 | tf_op jit(solution)/shard_map/all_gather | solution.py:68
  41.5 3.9 %copy.30 = bf16[2,512,1024]{1,2,0:T(8,128)(2,1)} copy(bf16[2,512,1024]{2,1,0:T(8,128)(2,1)} %bitcast.131) | data formatting | bytes 4194304 | tf_op jit(solution)/shard_map/reshape | solution.py:25
  45.5 8.3 %all_gather.16 = bf16[32,64,128]{2,1,0:T(8,128)(2,1)S(1)} all-gather(bf16[16,64,128]{2,1,0:T(8,128)(2,1)S(1)} %copy-done.10), channel_id=1, replica_groups=mesh['dp'=16,'tensor'=2] {'tensor'}, dimensions={0}, use_global_device_ids=true | all-gather | bytes 786432 | tf_op jit(solution)/shard_map/all_gather | solution.py:67
  53.8 13.1 %all_gather.17 = bf16[128,32,64]{2,1,0:T(8,128)(2,1)} all-gather(bf16[64,32,64]{2,1,0:T(8,128)(2,1)S(1)} %copy-done.9), channel_id=1, replica_groups=mesh['dp'=16,'tensor'=2] {'tensor'}, dimensions={0}, use_global_device_ids=true | all-gather | bytes 786432 | tf_op jit(solution)/shard_map/all_gather | solution.py:69
  66.8 7.2 %all_gather.19 = bf16[32,128,64]{1,2,0:T(8,128)(2,1)S(1)} all-gather(bf16[16,128,64]{1,2,0:T(8,128)(2,1)} %param.12), channel_id=1, replica_groups=mesh['dp'=16,'tensor'=2] {'tensor'}, dimensions={0}, use_global_device_ids=true | all-gather | bytes 786432 | tf_op jit(solution)/shard_map/all_gather | solution.py:72
  74.1 15.0 %all_gather.18 = bf16[128,64,32]{1,2,0:T(8,128)(2,1)} all-gather(bf16[64,64,32]{1,2,0:T(8,128)(2,1)} %param.11), channel_id=1, replica_groups=mesh['dp'=16,'tensor'=2] {'tensor'}, dimensions={0}, use_global_device_ids=true | all-gather | bytes 786432 | tf_op jit(solution)/shard_map/all_gather | solution.py:71
  89.1 4.8 %all-to-all-start.2 = ((bf16[2,512,1024]{1,2,0:T(8,128)(2,1)}), bf16[2,512,1024]{1,2,0:T(8,128)(2,1)}, u32[]{:S(2)}, u32[]{:S(2)}) async-start(bf16[2,512,1024]{1,2,0:T(8,128)(2,1)} %copy.30), calls=%async_computation.2 | async-start | bytes 4194304 | tf_op jit(solution)/shard_map/all_to_all | solution.py:25
  96.5 3.8 %convert_bitcast_fusion.4 = bf16[32,128,512]{1,2,0:T(8,128)(2,1)} fusion(bf16[32,64,128]{2,1,0:T(8,128)(2,1)S(1)} %all_gather.16, f32[32,64,512]{2,1,0:T(8,128)S(1)} %bitcast.119, f32[32,64]{1,0:T(8,128)S(1)} %mul.140, f32[512]{0:T(512)S(1)} %get-tuple-element.25, f32[512]{0:T(512)S(1)} %get-tuple-element.24), kind=kOutput, calls=%fused_computation.34 | convolution fusion | flops 274726912 | bytes 8925184 | tf_op jit(solution)/shard_map/ait,aim->amt/dot_general | solution.py:20
  100.3 7.9 %copy.27 = bf16[32,128,512]{2,0,1:T(8,128)(2,1)} copy(bf16[32,128,512]{1,2,0:T(8,128)(2,1)} %convert_bitcast_fusion.4) | data formatting | bytes 8388608 | tf_op jit(solution)/shard_map/convert_element_type | solution.py:81
  108.2 7.1 %all-to-all-done.2 = bf16[2,512,1024]{1,2,0:T(8,128)(2,1)} async-done(((bf16[2,512,1024]{1,2,0:T(8,128)(2,1)}), bf16[2,512,1024]{1,2,0:T(8,128)(2,1)}, u32[]{:S(2)}, u32[]{:S(2)}) %all-to-all-start.2) | async-done | bytes 2097184 | tf_op jit(solution)/shard_map/all_to_all | solution.py:25
  115.4 2.0 fusion.12
  117.4 1.3 copy-done.4
  118.7 3.3 convert_bitcast_fusion.2
  122.0 7.9 %copy.31 = bf16[128,32,512]{2,1,0:T(8,128)(2,1)} copy(bf16[128,32,512]{0,2,1:T(8,128)(2,1)} %convert_bitcast_fusion.2) | data formatting | bytes 8388608 | tf_op jit(solution)/shard_map/convert_element_type | solution.py:91
  129.9 10.3 %fusion.9 = (bf16[128,64,512]{2,1,0:T(8,128)(2,1)S(1)}, f32[128,512,64]{1,2,0:T(8,128)}) fusion(bf16[32,128,512]{2,0,1:T(8,128)(2,1)} %copy.27, bf16[128,32,64]{2,1,0:T(8,128)(2,1)} %all_gather.17), kind=kOutput, calls=%fused_computation.12 | convolution fusion | flops 289406976 | bytes 29884416 | tf_op jit(solution)/shard_map/amt,maq->mqt/dot_general | solution.py:20
  140.2 13.6 %fusion.5 = bf16[128,64,512]{2,1,0:T(8,128)(2,1)} fusion(f32[128,512,64]{1,2,0:T(8,128)} %get-tuple-element.28, bf16[128,32,512]{2,1,0:T(8,128)(2,1)S(1)} %copy-done.3, bf16[128,64,32]{1,2,0:T(8,128)(2,1)S(1)} %copy-done.7), kind=kOutput, calls=%fused_computation.6 | convolution fusion | flops 310378496 | bytes 29884416 | tf_op jit(solution)/shard_map/mpt,mqp->mqt/dot_general | solution.py:20
  153.8 6.7 %convolution_convert_fusion.1 = bf16[128,32,64]{2,1,0:T(8,128)(2,1)} fusion(bf16[32,128,512]{2,0,1:T(8,128)(2,1)S(1)} %copy-done, bf16[128,64,512]{2,1,0:T(8,128)(2,1)} %fusion.5), kind=kOutput, calls=%fused_computation.51 | convolution fusion | flops 268697600 | bytes 13107200 | tf_op jit(solution)/shard_map/amt,mqt->maq/dot_general | solution.py:20
  160.5 5.0 %convert_bitcast_fusion.1 = bf16[32,128,512]{2,0,1:T(8,128)(2,1)S(1)} fusion(bf16[128,32,64]{2,1,0:T(8,128)(2,1)} %all_gather.17, bf16[128,64,512]{2,1,0:T(8,128)(2,1)} %fusion.5), kind=kOutput, calls=%fused_computation.31 | convolution fusion | flops 270532608 | bytes 13107200 | tf_op jit(solution)/shard_map/mqt,maq->amt/dot_general | solution.py:20
  165.5 3.3 convolution_convert_fusion
  168.8 4.6 %convert_bitcast_fusion.3 = bf16[128,32,512]{2,1,0:T(8,128)(2,1)} fusion(bf16[128,64,32]{1,2,0:T(8,128)(2,1)} %all_gather.18, bf16[128,64,512]{2,1,0:T(8,128)(2,1)S(1)} %get-tuple-element.27), kind=kOutput, calls=%fused_computation.33 | convolution fusion | flops 270532608 | bytes 13107200 | tf_op jit(solution)/shard_map/mqt,mqp->mpt/dot_general | solution.py:20
  173.4 6.8 %fusion.37 = bf16[32,64,128]{2,1,0:T(8,128)(2,1)} fusion(bf16[32,128,512]{2,0,1:T(8,128)(2,1)S(1)} %convert_bitcast_fusion.1, f32[32,64,512]{2,1,0:T(8,128)S(1)} %bitcast.120, f32[32,64]{1,0:T(8,128)S(1)} %mul.140, f32[512]{0:T(512)S(1)} %copy-done.15, f32[512]{0:T(512)S(1)} %copy-done.12), kind=kOutput, calls=%fused_computation.53 | convolution fusion | flops 272891904 | bytes 8925184 | tf_op jit(solution)/shard_map/ait,amt->aim/dot_general | solution.py:20
  180.2 8.0 %fusion.13 = (f32[32,64]{1,0:T(8,128)}, f32[512]{0:T(512)}, f32[512]{0:T(512)}, f32[32,512,64]{1,2,0:T(8,128)}) fusion(f32[32,64,512]{2,1,0:T(8,128)S(1)} %bitcast.121, f32[512]{0:T(512)S(1)} %copy-done.15, f32[512]{0:T(512)S(1)} %copy-done.12, f32[32,64]{1,0:T(8,128)S(1)} %mul.140, bf16[32,64,128]{2,1,0:T(8,128)(2,1)S(1)} %all_gather.16, ...), kind=kOutput, calls=%fused_computation.20 | convolution fusion | flops 276820992 | bytes 13131776 | tf_op jit(solution)/shard_map/amt,aim->ait/dot_general | solution.py:20
  188.3 1.4 all_to_all.38
  189.7 3.2 all-to-all-start.8
  194.0 2.7 all-to-all-done.8
  196.7 3.5 all-to-all-start.5
  200.2 6.3 %fusion.34 = bf16[32,64,128]{2,1,0:T(8,128)(2,1)} fusion(bf16[32,64,512]{2,1,0:T(8,128)(2,1)} %bitcast.125, bf16[128,32,512]{2,1,0:T(8,128)(2,1)} %convert_bitcast_fusion.3), kind=kOutput, calls=%fused_computation.52 | convolution fusion | flops 268697600 | bytes 6815744 | tf_op jit(solution)/shard_map/mat,ait->aim/dot_general | solution.py:20
  206.7 4.2 %all-to-all-start.4 = ((bf16[2,1024,128]{2,1,0:T(8,128)(2,1)}), bf16[2,1024,128]{2,1,0:T(8,128)(2,1)}, u32[]{:S(2)}, u32[]{:S(2)}) async-start(bf16[2,1024,128]{2,1,0:T(8,128)(2,1)} %bitcast.135), calls=%async_computation.4 | async-start | bytes 1048576 | tf_op jit(solution)/shard_map/all_to_all | solution.py:54
  210.9 1.3 fusion.41
  213.3 4.4 %all-to-all-done.4 = bf16[2,1024,128]{2,1,0:T(8,128)(2,1)} async-done(((bf16[2,1024,128]{2,1,0:T(8,128)(2,1)}), bf16[2,1024,128]{2,1,0:T(8,128)(2,1)}, u32[]{:S(2)}, u32[]{:S(2)}) %all-to-all-start.4) | async-done | bytes 524320 | tf_op jit(solution)/shard_map/all_to_all | solution.py:54
  217.7 4.5 %all-to-all-start.6 = ((bf16[2,1024,128]{2,1,0:T(8,128)(2,1)}), bf16[2,1024,128]{2,1,0:T(8,128)(2,1)}, u32[]{:S(2)}, u32[]{:S(2)}) async-start(bf16[2,1024,128]{2,1,0:T(8,128)(2,1)} %bitcast.25), calls=%async_computation.6 | async-start | bytes 1048576 | tf_op jit(solution)/shard_map/all_to_all | solution.py:54
  222.3 9.0 %fusion.29 = f32[32,512,64]{1,2,0:T(8,128)} fusion(bf16[32,128,64]{1,2,0:T(8,128)(2,1)S(1)} %copy-done.6, bf16[128,32,512]{2,1,0:T(8,128)(2,1)} %convert_bitcast_fusion.3), kind=kOutput, calls=%fused_computation.47 | convolution fusion | flops 269484032 | bytes 8912896 | tf_op jit(solution)/shard_map/mat,ami->ait/dot_general | solution.py:20
  231.4 3.5 all-to-all-start.7
  234.9 6.2 %fusion.33 = (bf16[2,512,1024]{1,2,0:T(8,128)(2,1)}, bf16[2,512,1024]{1,2,0:T(8,128)(2,1)}) fusion(bf16[2,512,1024]{1,2,0:T(8,128)(2,1)S(1)} %all-to-all-done, f32[2,1024,512]{2,1,0:T(8,128)} %bitcast.123, bf16[2,512,1024]{1,2,0:T(8,128)(2,1)} %all-to-all-done.2, f32[512]{0:T(512)S(1)} %get-tuple-element.29, f32[512]{0:T(512)S(1)} %copy-done.13, ...), kind=kLoop, calls=%fused_computation.49 | loop fusion | flops 13631488 | bytes 16793600 | tf_op jit(solution)/shard_map/transpose | solution.py:31
  241.1 2.0 convert_reduce_fusion.4
  243.1 3.8 %all-to-all-start.3 = ((bf16[2,512,1024]{1,2,0:T(8,128)(2,1)}), bf16[2,512,1024]{1,2,0:T(8,128)(2,1)S(1)}, u32[]{:S(2)}, u32[]{:S(2)}) async-start(bf16[2,512,1024]{1,2,0:T(8,128)(2,1)} %get-tuple-element.14), calls=%async_computation.3 | async-start | bytes 4194304 | tf_op jit(solution)/shard_map/all_to_all | solution.py:32
  246.9 1.9 constant_dynamic-update-slice_fusion.4
  249.7 1.2 convert_reduce_fusion.2
  253.2 12.2 %all-to-all-done.3 = bf16[2,512,1024]{1,2,0:T(8,128)(2,1)S(1)} async-done(((bf16[2,512,1024]{1,2,0:T(8,128)(2,1)}), bf16[2,512,1024]{1,2,0:T(8,128)(2,1)S(1)}, u32[]{:S(2)}, u32[]{:S(2)}) %all-to-all-start.3) | async-done | bytes 2097184 | tf_op jit(solution)/shard_map/all_to_all | solution.py:32
  265.4 4.8 %all-to-all-start.1 = ((bf16[2,512,1024]{1,2,0:T(8,128)(2,1)}), bf16[2,512,1024]{1,2,0:T(8,128)(2,1)}, u32[]{:S(2)}, u32[]{:S(2)}) async-start(bf16[2,512,1024]{1,2,0:T(8,128)(2,1)} %get-tuple-element.15), calls=%async_computation.1 | async-start | bytes 4194304 | tf_op jit(solution)/shard_map/all_to_all | solution.py:32
  270.2 2.4 copy.33
  272.6 14.7 %all-to-all-done.1 = bf16[2,512,1024]{1,2,0:T(8,128)(2,1)} async-done(((bf16[2,512,1024]{1,2,0:T(8,128)(2,1)}), bf16[2,512,1024]{1,2,0:T(8,128)(2,1)}, u32[]{:S(2)}, u32[]{:S(2)}) %all-to-all-start.1) | async-done | bytes 2097184 | tf_op jit(solution)/shard_map/all_to_all | solution.py:32
  287.3 3.9 %copy.29 = bf16[2,512,1024]{2,1,0:T(8,128)(2,1)} copy(bf16[2,512,1024]{1,2,0:T(8,128)(2,1)} %all-to-all-done.1) | data formatting | bytes 4194304 | tf_op jit(solution)/shard_map/all_to_all | solution.py:32
  291.2 61.4 %all-reduce.2.cloned.1.call-done = f32[4104,128]{1,0:T(8,128)} async-done(((f32[4104,128]{1,0:T(8,128)}), f32[4104,128]{1,0:T(8,128)}) %all-reduce.2.cloned.1.call-update) | async-done | bytes 2101264 | tf_op jit(solution)/shard_map/psum | solution.py:107
  352.6 1.7 broadcast_multiply_fusion
  356.5 1.6 pad_maximum_fusion
  (66 shorter events, 10.7 us)
Async XLA Ops:
  7.2 8.3 %copy-start.19 = (bf16[1024]{0:T(1024)(128)(2,1)S(1)}, bf16[1024]{0:T(1024)(128)(2,1)}, u32[]{:S(2)}) copy-start(bf16[1024]{0:T(1024)(128)(2,1)} %param.8) | copy-start | bytes 6148
  11.1 34.3 %copy-start.10 = (bf16[16,64,128]{2,1,0:T(8,128)(2,1)S(1)}, bf16[16,64,128]{2,1,0:T(8,128)(2,1)}, u32[]{:S(2)}) copy-start(bf16[16,64,128]{2,1,0:T(8,128)(2,1)} %param.9) | copy-start | bytes 786436
  11.1 42.6 %copy-start.9 = (bf16[64,32,64]{2,1,0:T(8,128)(2,1)S(1)}, bf16[64,32,64]{2,1,0:T(8,128)(2,1)}, u32[]{:S(2)}) copy-start(bf16[64,32,64]{2,1,0:T(8,128)(2,1)} %param.10) | copy-start | bytes 786436
  11.1 78.0 %all-to-all-start = ((bf16[2,512,1024]{1,2,0:T(8,128)(2,1)}), bf16[2,512,1024]{1,2,0:T(8,128)(2,1)S(1)}, u32[]{:S(2)}, u32[]{:S(2)}) async-start(bf16[2,512,1024]{1,2,0:T(8,128)(2,1)} %copy.26), calls=%async_computation | async-start | bytes 4194304 | tf_op jit(solution)/shard_map/all_to_all | solution.py:25
  74.1 43.3 %copy-start.5 = (bf16[32,128,64]{1,2,0:T(8,128)(2,1)}, bf16[32,128,64]{1,2,0:T(8,128)(2,1)S(1)}, u32[]{:S(2)}) copy-start(bf16[32,128,64]{1,2,0:T(8,128)(2,1)S(1)} %all_gather.19) | copy-start | bytes 1572868
  89.1 26.3 %all-to-all-start.2 = ((bf16[2,512,1024]{1,2,0:T(8,128)(2,1)}), bf16[2,512,1024]{1,2,0:T(8,128)(2,1)}, u32[]{:S(2)}, u32[]{:S(2)}) async-start(bf16[2,512,1024]{1,2,0:T(8,128)(2,1)} %copy.30), calls=%async_computation.2 | async-start | bytes 4194304 | tf_op jit(solution)/shard_map/all_to_all | solution.py:25
  94.5 2.0 copy-start.1
  95.4 4.9 %copy-start.11 = (f32[512]{0:T(512)}, f32[512]{0:T(512)S(1)}, u32[]{:S(2)}) copy-start(f32[512]{0:T(512)S(1)} %get-tuple-element.24) | copy-start | bytes 6148
  95.4 4.9 %copy-start.14 = (f32[512]{0:T(512)}, f32[512]{0:T(512)S(1)}, u32[]{:S(2)}) copy-start(f32[512]{0:T(512)S(1)} %get-tuple-element.25) | copy-start | bytes 6148
  117.4 1.3 copy-start.4
  129.9 10.3 %copy-start.3 = (bf16[128,32,512]{2,1,0:T(8,128)(2,1)S(1)}, bf16[128,32,512]{2,1,0:T(8,128)(2,1)}, u32[]{:S(2)}) copy-start(bf16[128,32,512]{2,1,0:T(8,128)(2,1)} %copy.31) | copy-start | bytes 12582916
  129.9 10.3 %copy-start.7 = (bf16[128,64,32]{1,2,0:T(8,128)(2,1)S(1)}, bf16[128,64,32]{1,2,0:T(8,128)(2,1)}, u32[]{:S(2)}) copy-start(bf16[128,64,32]{1,2,0:T(8,128)(2,1)} %all_gather.18) | copy-start | bytes 1572868
  140.2 13.6 %copy-start = (bf16[32,128,512]{2,0,1:T(8,128)(2,1)S(1)}, bf16[32,128,512]{2,0,1:T(8,128)(2,1)}, u32[]{:S(2)}) copy-start(bf16[32,128,512]{2,0,1:T(8,128)(2,1)} %copy.27) | copy-start | bytes 12582916
  168.8 4.7 %copy-start.2 = (f32[2,512,1024]{1,2,0:T(8,128)S(1)}, f32[2,512,1024]{1,2,0:T(8,128)}, u32[]{:S(2)}) copy-start(f32[2,512,1024]{1,2,0:T(8,128)} %copy-done.1) | copy-start | bytes 12582916
  168.8 4.7 %copy-start.12 = (f32[512]{0:T(512)S(1)}, f32[512]{0:T(512)}, u32[]{:S(2)}) copy-start(f32[512]{0:T(512)} %copy-done.11) | copy-start | bytes 6148
  168.8 4.7 %copy-start.15 = (f32[512]{0:T(512)S(1)}, f32[512]{0:T(512)}, u32[]{:S(2)}) copy-start(f32[512]{0:T(512)} %copy-done.14) | copy-start | bytes 6148
  180.2 8.0 %copy-start.8 = (bf16[128,32,64]{2,1,0:T(8,128)(2,1)S(1)}, bf16[128,32,64]{2,1,0:T(8,128)(2,1)}, u32[]{:S(2)}) copy-start(bf16[128,32,64]{2,1,0:T(8,128)(2,1)} %convolution_convert_fusion.1) | copy-start | bytes 1572868
  189.7 7.0 %all-to-all-start.8 = ((f32[2,1,1024]{2,1,0:T(1,128)}), f32[2,1,1024]{2,1,0:T(1,128)S(1)}, u32[]{:S(2)}, u32[]{:S(2)}) async-start(f32[2,1,1024]{2,1,0:T(1,128)} %all_to_all.38), calls=%async_computation.8 | async-start | bytes 16384 | tf_op jit(solution)/shard_map/all_to_all | solution.py:104
  196.7 10.1 %all-to-all-start.5 = ((bf16[2,1024,128]{2,1,0:T(8,128)(2,1)}), bf16[2,1024,128]{2,1,0:T(8,128)(2,1)S(1)}, u32[]{:S(2)}, u32[]{:S(2)}) async-start(bf16[2,1024,128]{2,1,0:T(8,128)(2,1)} %bitcast.23), calls=%async_computation.5 | async-start | bytes 1048576 | tf_op jit(solution)/shard_map/all_to_all | solution.py:54
  206.4 15.8 %copy-start.6 = (bf16[32,128,64]{1,2,0:T(8,128)(2,1)S(1)}, bf16[32,128,64]{1,2,0:T(8,128)(2,1)}, u32[]{:S(2)}) copy-start(bf16[32,128,64]{1,2,0:T(8,128)(2,1)} %copy-done.5) | copy-start | bytes 1572868
  206.7 11.0 %all-to-all-start.4 = ((bf16[2,1024,128]{2,1,0:T(8,128)(2,1)}), bf16[2,1024,128]{2,1,0:T(8,128)(2,1)}, u32[]{:S(2)}, u32[]{:S(2)}) async-start(bf16[2,1024,128]{2,1,0:T(8,128)(2,1)} %bitcast.135), calls=%async_computation.4 | async-start | bytes 1048576 | tf_op jit(solution)/shard_map/all_to_all | solution.py:54
  217.7 13.6 %all-to-all-start.6 = ((bf16[2,1024,128]{2,1,0:T(8,128)(2,1)}), bf16[2,1024,128]{2,1,0:T(8,128)(2,1)}, u32[]{:S(2)}, u32[]{:S(2)}) async-start(bf16[2,1024,128]{2,1,0:T(8,128)(2,1)} %bitcast.25), calls=%async_computation.6 | async-start | bytes 1048576 | tf_op jit(solution)/shard_map/all_to_all | solution.py:54
  222.2 9.1 %copy-start.17 = (f32[512]{0:T(512)S(1)}, f32[512]{0:T(512)}, u32[]{:S(2)}) copy-start(f32[512]{0:T(512)} %get-tuple-element.8) | copy-start | bytes 6148
  222.3 9.1 %copy-start.18 = (f32[512]{0:T(512)S(1)}, f32[512]{0:T(512)}, u32[]{:S(2)}) copy-start(f32[512]{0:T(512)} %get-tuple-element.9) | copy-start | bytes 6148
  222.3 12.6 %copy-start.13 = (f32[512]{0:T(512)S(1)}, f32[512]{0:T(512)}, u32[]{:S(2)}) copy-start(f32[512]{0:T(512)} %copy-done.11) | copy-start | bytes 6148
  222.3 12.6 %copy-start.16 = (f32[512]{0:T(512)S(1)}, f32[512]{0:T(512)}, u32[]{:S(2)}) copy-start(f32[512]{0:T(512)} %copy-done.14) | copy-start | bytes 6148
  231.4 11.8 %all-to-all-start.7 = ((bf16[2,1024,128]{2,1,0:T(8,128)(2,1)}), bf16[2,1024,128]{2,1,0:T(8,128)(2,1)S(1)}, u32[]{:S(2)}, u32[]{:S(2)}) async-start(bf16[2,1024,128]{2,1,0:T(8,128)(2,1)} %bitcast.134), calls=%async_computation.7 | async-start | bytes 1048576 | tf_op jit(solution)/shard_map/all_to_all | solution.py:54
  243.1 22.3 %all-to-all-start.3 = ((bf16[2,512,1024]{1,2,0:T(8,128)(2,1)}), bf16[2,512,1024]{1,2,0:T(8,128)(2,1)S(1)}, u32[]{:S(2)}, u32[]{:S(2)}) async-start(bf16[2,512,1024]{1,2,0:T(8,128)(2,1)} %get-tuple-element.14), calls=%async_computation.3 | async-start | bytes 4194304 | tf_op jit(solution)/shard_map/all_to_all | solution.py:32
  246.9 105.7 %all-reduce.2.cloned.1.call-start = ((), (), s32[]{:S(2)}) async-start(), calls=%async_computation.9 | async-start | bytes 4202496 | tf_op jit(solution)/shard_map/psum | solution.py:107
  265.4 21.9 %all-to-all-start.1 = ((bf16[2,512,1024]{1,2,0:T(8,128)(2,1)}), bf16[2,512,1024]{1,2,0:T(8,128)(2,1)}, u32[]{:S(2)}, u32[]{:S(2)}) async-start(bf16[2,512,1024]{1,2,0:T(8,128)(2,1)} %get-tuple-element.15), calls=%async_computation.1 | async-start | bytes 4194304 | tf_op jit(solution)/shard_map/all_to_all | solution.py:32
Sparse Core Ops, SparseCore 0:
  253.4 99.2 all-reduce.1
